TPU v7x, 128 devices: a whole 4x4x4 slice. The times are simulated.
128 devices in a mesh: blk: 16 (over y, x), sims: 8 (over z, core).
Axes of the slice: x: 4, y: 4, z: 4, core: 2. Of those that a mesh axis runs over, the one named last changes fastest.
Arguments:
- rhs: float32 [4, 16, 256, 1024], P(None, 'blk', None, 'sims'), parts along dimension 3, may hold values from -6 to 6
- lower_blocks: float32 [4, 16, 3, 256, 256], P(None, 'blk'), may hold values from -0.16875 to 0.16875
- col_index: int32 [4, 16, 3], P(None, 'blk'), may hold values from -1 to 62, as said below
- diag_inverse: float32 [4, 16, 256, 256], P(None, 'blk'), may hold values from -1.5 to 1.5, as said below
- turnout: float32 [4, 16, 256], P(None, 'blk'), may hold values from 0.2 to 5
- district_of: int32 [4, 16, 256], P(None, 'blk'), may hold values from 0 to 255, as said below
Outputs:
- solution: float32 [4, 16, 256, 1024], P(None, 'blk', None, 'sims'), parts along dimension 3
- district_mean: float32 [256, 1024], P('blk', 'sims'), parts along dimension 1
There are 8 independent parts, one for each index of `sims`. A program takes and returns all parts, laid end to end along the dimension named above; an argument that names none is the same for every part. Nothing has to cross between parts.
Inputs may be any that keep to these rules, and one draw needn't show every extreme that they name: `col_index`: entry [r, p, k] belongs to block row i = r * 16 + p. Slot 0 holds i - 1 (-1 for i = 0); the other slots hold distinct columns from i - 4 to i - 2, or -1 where the block is absent. `diag_inverse`: each block is lower triangular. `district_of`: each district holds exactly 64 precincts.
All inputs are finite; a program needn't handle non-finite values.
Results may differ from a plain program's by a relative error of at most 0.0002.
Values sent between devices are 32-bit elements; how exact they have to be, the bound alone decides.
A program may use at most 64 MiB of HBM per device.

v0:
```python
import jax
import jax.numpy as jnp
from jax import lax
from jax.sharding import PartitionSpec as P

WIN = 4
NDIST = 256


precise = lax.Precision.HIGHEST


def shifted(value, axis, by):
    size = lax.axis_size(axis)
    return lax.ppermute(value, axis, [(i, (i + by) % size) for i in range(size)])


def body(rhs, lower_blocks, col_index, diag_inverse, turnout, district_of):
    cycle_size = lax.axis_size("blk")
    device_index = lax.axis_index("blk")
    rows_here = rhs.shape[0]
    total_rows = rows_here * cycle_size
    block_size = rhs.shape[2]
    columns = rhs.shape[3]
    local_rhs = rhs[:, 0]
    factor = lower_blocks[:, 0]
    pattern = col_index[:, 0]
    inverses = diag_inverse[:, 0]
    piece_count = 1
    piece_width = columns // piece_count
    window_slots = jnp.arange(WIN, dtype=jnp.int32)
    zero_index = jnp.zeros((), jnp.int32)

    def advance(wave_step, loop_state):
        pending, solution = loop_state
        lead_row = (total_rows - 1 - wave_step).astype(jnp.int32)
        piece_now = jnp.mod(device_index - lead_row, cycle_size)
        row_now = lead_row + piece_now
        is_valid = (piece_now < piece_count) & (row_now >= 0) & (row_now <= total_rows - 1)
        row_safe = jnp.clip(row_now, 0, total_rows - 1)
        slot_now = row_safe // cycle_size
        start_col = jnp.minimum(piece_now, piece_count - 1) * piece_width
        pending = jnp.where(row_now == total_rows - 1, jnp.zeros_like(pending), pending)
        source = lax.dynamic_slice(
            local_rhs, (slot_now, zero_index, start_col), (1, block_size, piece_width)
        )[0]
        inverse_now = lax.dynamic_index_in_dim(inverses, slot_now, 0, keepdims=False)
        solved = jnp.einsum("ab,as->bs", inverse_now, source - pending[0], precision=precise)
        blocks_now = lax.dynamic_index_in_dim(factor, slot_now, 0, keepdims=False)
        columns_now = lax.dynamic_index_in_dim(pattern, slot_now, 0, keepdims=False)
        present = columns_now >= 0
        updates = jnp.einsum("kab,as->kbs", blocks_now, solved, precision=precise)
        target = row_safe - 1 - columns_now
        routing = (present[:, None] & (target[:, None] == window_slots[None, :])).astype(
            jnp.float32
        )
        added_terms = jnp.einsum("kw,kbs->wbs", routing, updates, precision=precise)
        moved_carry = jnp.concatenate([pending[1:], jnp.zeros_like(pending[:1])], 0) + added_terms
        old_piece = lax.dynamic_slice(
            solution, (slot_now, zero_index, start_col), (1, block_size, piece_width)
        )
        kept_piece = jnp.where(is_valid, solved[None], old_piece)
        solution = lax.dynamic_update_slice(solution, kept_piece, (slot_now, zero_index, start_col))
        pending = shifted(moved_carry, "blk", -1)
        return (pending, solution)

    start_carry = jnp.zeros((WIN, block_size, piece_width), jnp.float32)
    start_field = jnp.zeros_like(local_rhs)
    _, solution = lax.fori_loop(
        0, total_rows + piece_count - 1, advance, (start_carry, start_field)
    )
    cell_rows = solution.reshape(rows_here * block_size, columns)
    weights = turnout[:, 0].reshape(rows_here * block_size)
    district_ids = district_of[:, 0].reshape(rows_here * block_size)
    member = (district_ids[:, None] == jnp.arange(NDIST, dtype=jnp.int32)[None, :]).astype(
        jnp.float32
    )
    numerator = jnp.einsum("cd,cs->ds", member, weights[:, None] * cell_rows, precision=precise)
    denominator = jnp.einsum("cd,c->d", member, weights, precision=precise)
    numer_share, denom_share = (
        lax.psum_scatter(numerator, "blk", scatter_dimension=0, tiled=True),
        lax.psum_scatter(denominator, "blk", scatter_dimension=0, tiled=True),
    )
    return (solution[:, None], numer_share / denom_share[:, None])


def solution(mesh):
    placed = (
        P(None, "blk", None, "sims"),
        P(None, "blk", None, None, None),
        P(None, "blk", None),
        P(None, "blk", None, None),
        P(None, "blk", None),
        P(None, "blk", None),
    )
    return jax.shard_map(
        body,
        mesh=mesh,
        in_specs=placed,
        out_specs=(P(None, "blk", None, "sims"), P("blk", "sims")),
        check_vma=False,
    )
```

profile of v0, /device:TPU:1, one launch (start us, length us, event | category | flops | bytes accessed | tf_op | source)
XLA Modules:
  0.0 1360.6 jit_solution(3338090997867300478)
XLA Ops:
  9.5 1191.1 %while.19 = (s32[]{:T(128)}, f32[4,256,128]{2,0,1:T(4,128)S(1)}, f32[4,256,128]{2,1,0:T(8,128)S(1)}, s32[]{:T(128)}, s32[4,3]{1,0:T(4,128)S(1)}, /*index=5*/f32[...) while((s32[]{:T(128)}, f32[4,256,128]{2,0,1:T(4,128)S(1)}, ...), condition=%wide.region_1.2_spmd.clone, body=%wide.region_0.1_spmd.clone.sunk | while | flops 407699520 | bytes 7735375 | solution.py:69
  20.8 10.6 collective-permute-done
  42.4 9.7 collective-permute-done
  63.1 8.7 collective-permute-done
  274.9 9.6 collective-permute-done
  295.2 10.7 collective-permute-done
  316.6 11.7 collective-permute-done
  339.2 10.8 collective-permute-done
  361.0 9.9 collective-permute-done
  381.9 9.0 collective-permute-done
  593.7 9.2 collective-permute-done
  613.6 10.3 collective-permute-done
  634.6 11.4 collective-permute-done
  656.8 10.9 collective-permute-done
  678.7 10.0 collective-permute-done
  699.7 9.1 collective-permute-done
  911.8 9.1 collective-permute-done
  931.6 10.2 collective-permute-done
  952.5 11.2 collective-permute-done
  974.4 11.1 collective-permute-done
  996.5 10.1 collective-permute-done
  1017.6 9.2 collective-permute-done
  1204.5 34.1 %all-reduce.2 = f32[256]{0:T(256)S(1)} all-reduce(f32[256]{0:T(256)S(1)} %bitcast.69), channel_id=3, replica_groups=mesh['blk'=16,'sims'=8] {'blk'}, use_global_device_ids=true, to_apply=%region_3.4.clone | all-reduce | flops 256 | bytes 2048
  1238.6 113.7 %all-reduce.5.cloned.1.call-done = f32[256,128]{1,0:T(8,128)} async-done(((f32[256,128]{1,0:T(8,128)}), f32[256,128]{1,0:T(8,128)}) %all-reduce.5.cloned.1.call-update) | async-done | bytes 131088
  (639 shorter events, 981.1 us)
Async XLA Ops:
  7.2 1345.2 %all-reduce.5.cloned.1.call-start = ((), (), s32[]{:S(2)}) async-start(), calls=%async_computation | async-start | bytes 262144
  15.0 16.4 %collective-permute-start = (f32[4,256,128]{2,0,1:T(4,128)S(1)}, f32[4,256,128]{2,0,1:T(4,128)S(1)}, u32[]{:S(2)}, u32[]{:S(2)}) collective-permute-start(f32[4,256,128]{2,0,1:T(4,128)S(1)} %convolution_add_fusion.2), channel_id=1, source_target_pairs={{0,120},{8,0},{16,8},{24,16},{32,24},{40,32},{48,40},{56,48},{64,5... | collective-permute-start | bytes 1572872 | tf_op jit(solution)/shard_map/while/body/eval_jaxpr/ppermute | solution.py:15
  36.8 15.3 %collective-permute-start = (f32[4,256,128]{2,0,1:T(4,128)S(1)}, f32[4,256,128]{2,0,1:T(4,128)S(1)}, u32[]{:S(2)}, u32[]{:S(2)}) collective-permute-start(f32[4,256,128]{2,0,1:T(4,128)S(1)} %convolution_add_fusion.2), channel_id=1, source_target_pairs={{0,120},{8,0},{16,8},{24,16},{32,24},{40,32},{48,40},{56,48},{64,5... | collective-permute-start | bytes 1572872 | tf_op jit(solution)/shard_map/while/body/eval_jaxpr/ppermute | solution.py:15
  57.5 14.3 %collective-permute-start = (f32[4,256,128]{2,0,1:T(4,128)S(1)}, f32[4,256,128]{2,0,1:T(4,128)S(1)}, u32[]{:S(2)}, u32[]{:S(2)}) collective-permute-start(f32[4,256,128]{2,0,1:T(4,128)S(1)} %convolution_add_fusion.2), channel_id=1, source_target_pairs={{0,120},{8,0},{16,8},{24,16},{32,24},{40,32},{48,40},{56,48},{64,5... | collective-permute-start | bytes 1572872 | tf_op jit(solution)/shard_map/while/body/eval_jaxpr/ppermute | solution.py:15
  250.3 13.8 %collective-permute-start = (f32[4,256,128]{2,0,1:T(4,128)S(1)}, f32[4,256,128]{2,0,1:T(4,128)S(1)}, u32[]{:S(2)}, u32[]{:S(2)}) collective-permute-start(f32[4,256,128]{2,0,1:T(4,128)S(1)} %convolution_add_fusion.2), channel_id=1, source_target_pairs={{0,120},{8,0},{16,8},{24,16},{32,24},{40,32},{48,40},{56,48},{64,5... | collective-permute-start | bytes 1572872 | tf_op jit(solution)/shard_map/while/body/eval_jaxpr/ppermute | solution.py:15
  269.6 14.9 %collective-permute-start = (f32[4,256,128]{2,0,1:T(4,128)S(1)}, f32[4,256,128]{2,0,1:T(4,128)S(1)}, u32[]{:S(2)}, u32[]{:S(2)}) collective-permute-start(f32[4,256,128]{2,0,1:T(4,128)S(1)} %convolution_add_fusion.2), channel_id=1, source_target_pairs={{0,120},{8,0},{16,8},{24,16},{32,24},{40,32},{48,40},{56,48},{64,5... | collective-permute-start | bytes 1572872 | tf_op jit(solution)/shard_map/while/body/eval_jaxpr/ppermute | solution.py:15
  289.9 16.0 %collective-permute-start = (f32[4,256,128]{2,0,1:T(4,128)S(1)}, f32[4,256,128]{2,0,1:T(4,128)S(1)}, u32[]{:S(2)}, u32[]{:S(2)}) collective-permute-start(f32[4,256,128]{2,0,1:T(4,128)S(1)} %convolution_add_fusion.2), channel_id=1, source_target_pairs={{0,120},{8,0},{16,8},{24,16},{32,24},{40,32},{48,40},{56,48},{64,5... | collective-permute-start | bytes 1572872 | tf_op jit(solution)/shard_map/while/body/eval_jaxpr/ppermute | solution.py:15
  311.3 17.0 %collective-permute-start = (f32[4,256,128]{2,0,1:T(4,128)S(1)}, f32[4,256,128]{2,0,1:T(4,128)S(1)}, u32[]{:S(2)}, u32[]{:S(2)}) collective-permute-start(f32[4,256,128]{2,0,1:T(4,128)S(1)} %convolution_add_fusion.2), channel_id=1, source_target_pairs={{0,120},{8,0},{16,8},{24,16},{32,24},{40,32},{48,40},{56,48},{64,5... | collective-permute-start | bytes 1572872 | tf_op jit(solution)/shard_map/while/body/eval_jaxpr/ppermute | solution.py:15
  333.6 16.4 %collective-permute-start = (f32[4,256,128]{2,0,1:T(4,128)S(1)}, f32[4,256,128]{2,0,1:T(4,128)S(1)}, u32[]{:S(2)}, u32[]{:S(2)}) collective-permute-start(f32[4,256,128]{2,0,1:T(4,128)S(1)} %convolution_add_fusion.2), channel_id=1, source_target_pairs={{0,120},{8,0},{16,8},{24,16},{32,24},{40,32},{48,40},{56,48},{64,5... | collective-permute-start | bytes 1572872 | tf_op jit(solution)/shard_map/while/body/eval_jaxpr/ppermute | solution.py:15
  355.4 15.5 %collective-permute-start = (f32[4,256,128]{2,0,1:T(4,128)S(1)}, f32[4,256,128]{2,0,1:T(4,128)S(1)}, u32[]{:S(2)}, u32[]{:S(2)}) collective-permute-start(f32[4,256,128]{2,0,1:T(4,128)S(1)} %convolution_add_fusion.2), channel_id=1, source_target_pairs={{0,120},{8,0},{16,8},{24,16},{32,24},{40,32},{48,40},{56,48},{64,5... | collective-permute-start | bytes 1572872 | tf_op jit(solution)/shard_map/while/body/eval_jaxpr/ppermute | solution.py:15
  376.3 14.5 %collective-permute-start = (f32[4,256,128]{2,0,1:T(4,128)S(1)}, f32[4,256,128]{2,0,1:T(4,128)S(1)}, u32[]{:S(2)}, u32[]{:S(2)}) collective-permute-start(f32[4,256,128]{2,0,1:T(4,128)S(1)} %convolution_add_fusion.2), channel_id=1, source_target_pairs={{0,120},{8,0},{16,8},{24,16},{32,24},{40,32},{48,40},{56,48},{64,5... | collective-permute-start | bytes 1572872 | tf_op jit(solution)/shard_map/while/body/eval_jaxpr/ppermute | solution.py:15
  588.4 14.5 %collective-permute-start = (f32[4,256,128]{2,0,1:T(4,128)S(1)}, f32[4,256,128]{2,0,1:T(4,128)S(1)}, u32[]{:S(2)}, u32[]{:S(2)}) collective-permute-start(f32[4,256,128]{2,0,1:T(4,128)S(1)} %convolution_add_fusion.2), channel_id=1, source_target_pairs={{0,120},{8,0},{16,8},{24,16},{32,24},{40,32},{48,40},{56,48},{64,5... | collective-permute-start | bytes 1572872 | tf_op jit(solution)/shard_map/while/body/eval_jaxpr/ppermute | solution.py:15
  608.3 15.6 %collective-permute-start = (f32[4,256,128]{2,0,1:T(4,128)S(1)}, f32[4,256,128]{2,0,1:T(4,128)S(1)}, u32[]{:S(2)}, u32[]{:S(2)}) collective-permute-start(f32[4,256,128]{2,0,1:T(4,128)S(1)} %convolution_add_fusion.2), channel_id=1, source_target_pairs={{0,120},{8,0},{16,8},{24,16},{32,24},{40,32},{48,40},{56,48},{64,5... | collective-permute-start | bytes 1572872 | tf_op jit(solution)/shard_map/while/body/eval_jaxpr/ppermute | solution.py:15
  629.4 16.7 %collective-permute-start = (f32[4,256,128]{2,0,1:T(4,128)S(1)}, f32[4,256,128]{2,0,1:T(4,128)S(1)}, u32[]{:S(2)}, u32[]{:S(2)}) collective-permute-start(f32[4,256,128]{2,0,1:T(4,128)S(1)} %convolution_add_fusion.2), channel_id=1, source_target_pairs={{0,120},{8,0},{16,8},{24,16},{32,24},{40,32},{48,40},{56,48},{64,5... | collective-permute-start | bytes 1572872 | tf_op jit(solution)/shard_map/while/body/eval_jaxpr/ppermute | solution.py:15
  651.5 16.2 %collective-permute-start = (f32[4,256,128]{2,0,1:T(4,128)S(1)}, f32[4,256,128]{2,0,1:T(4,128)S(1)}, u32[]{:S(2)}, u32[]{:S(2)}) collective-permute-start(f32[4,256,128]{2,0,1:T(4,128)S(1)} %convolution_add_fusion.2), channel_id=1, source_target_pairs={{0,120},{8,0},{16,8},{24,16},{32,24},{40,32},{48,40},{56,48},{64,5... | collective-permute-start | bytes 1572872 | tf_op jit(solution)/shard_map/while/body/eval_jaxpr/ppermute | solution.py:15
  673.1 15.6 %collective-permute-start = (f32[4,256,128]{2,0,1:T(4,128)S(1)}, f32[4,256,128]{2,0,1:T(4,128)S(1)}, u32[]{:S(2)}, u32[]{:S(2)}) collective-permute-start(f32[4,256,128]{2,0,1:T(4,128)S(1)} %convolution_add_fusion.2), channel_id=1, source_target_pairs={{0,120},{8,0},{16,8},{24,16},{32,24},{40,32},{48,40},{56,48},{64,5... | collective-permute-start | bytes 1572872 | tf_op jit(solution)/shard_map/while/body/eval_jaxpr/ppermute | solution.py:15
  694.1 14.7 %collective-permute-start = (f32[4,256,128]{2,0,1:T(4,128)S(1)}, f32[4,256,128]{2,0,1:T(4,128)S(1)}, u32[]{:S(2)}, u32[]{:S(2)}) collective-permute-start(f32[4,256,128]{2,0,1:T(4,128)S(1)} %convolution_add_fusion.2), channel_id=1, source_target_pairs={{0,120},{8,0},{16,8},{24,16},{32,24},{40,32},{48,40},{56,48},{64,5... | collective-permute-start | bytes 1572872 | tf_op jit(solution)/shard_map/while/body/eval_jaxpr/ppermute | solution.py:15
  906.5 14.4 %collective-permute-start = (f32[4,256,128]{2,0,1:T(4,128)S(1)}, f32[4,256,128]{2,0,1:T(4,128)S(1)}, u32[]{:S(2)}, u32[]{:S(2)}) collective-permute-start(f32[4,256,128]{2,0,1:T(4,128)S(1)} %convolution_add_fusion.2), channel_id=1, source_target_pairs={{0,120},{8,0},{16,8},{24,16},{32,24},{40,32},{48,40},{56,48},{64,5... | collective-permute-start | bytes 1572872 | tf_op jit(solution)/shard_map/while/body/eval_jaxpr/ppermute | solution.py:15
  926.3 15.5 %collective-permute-start = (f32[4,256,128]{2,0,1:T(4,128)S(1)}, f32[4,256,128]{2,0,1:T(4,128)S(1)}, u32[]{:S(2)}, u32[]{:S(2)}) collective-permute-start(f32[4,256,128]{2,0,1:T(4,128)S(1)} %convolution_add_fusion.2), channel_id=1, source_target_pairs={{0,120},{8,0},{16,8},{24,16},{32,24},{40,32},{48,40},{56,48},{64,5... | collective-permute-start | bytes 1572872 | tf_op jit(solution)/shard_map/while/body/eval_jaxpr/ppermute | solution.py:15
  947.2 16.5 %collective-permute-start = (f32[4,256,128]{2,0,1:T(4,128)S(1)}, f32[4,256,128]{2,0,1:T(4,128)S(1)}, u32[]{:S(2)}, u32[]{:S(2)}) collective-permute-start(f32[4,256,128]{2,0,1:T(4,128)S(1)} %convolution_add_fusion.2), channel_id=1, source_target_pairs={{0,120},{8,0},{16,8},{24,16},{32,24},{40,32},{48,40},{56,48},{64,5... | collective-permute-start | bytes 1572872 | tf_op jit(solution)/shard_map/while/body/eval_jaxpr/ppermute | solution.py:15
  969.1 16.4 %collective-permute-start = (f32[4,256,128]{2,0,1:T(4,128)S(1)}, f32[4,256,128]{2,0,1:T(4,128)S(1)}, u32[]{:S(2)}, u32[]{:S(2)}) collective-permute-start(f32[4,256,128]{2,0,1:T(4,128)S(1)} %convolution_add_fusion.2), channel_id=1, source_target_pairs={{0,120},{8,0},{16,8},{24,16},{32,24},{40,32},{48,40},{56,48},{64,5... | collective-permute-start | bytes 1572872 | tf_op jit(solution)/shard_map/while/body/eval_jaxpr/ppermute | solution.py:15
  990.9 15.7 %collective-permute-start = (f32[4,256,128]{2,0,1:T(4,128)S(1)}, f32[4,256,128]{2,0,1:T(4,128)S(1)}, u32[]{:S(2)}, u32[]{:S(2)}) collective-permute-start(f32[4,256,128]{2,0,1:T(4,128)S(1)} %convolution_add_fusion.2), channel_id=1, source_target_pairs={{0,120},{8,0},{16,8},{24,16},{32,24},{40,32},{48,40},{56,48},{64,5... | collective-permute-start | bytes 1572872 | tf_op jit(solution)/shard_map/while/body/eval_jaxpr/ppermute | solution.py:15
  1012.0 14.8 %collective-permute-start = (f32[4,256,128]{2,0,1:T(4,128)S(1)}, f32[4,256,128]{2,0,1:T(4,128)S(1)}, u32[]{:S(2)}, u32[]{:S(2)}) collective-permute-start(f32[4,256,128]{2,0,1:T(4,128)S(1)} %convolution_add_fusion.2), channel_id=1, source_target_pairs={{0,120},{8,0},{16,8},{24,16},{32,24},{40,32},{48,40},{56,48},{64,5... | collective-permute-start | bytes 1572872 | tf_op jit(solution)/shard_map/while/body/eval_jaxpr/ppermute | solution.py:15
  1032.2 13.9 %collective-permute-start = (f32[4,256,128]{2,0,1:T(4,128)S(1)}, f32[4,256,128]{2,0,1:T(4,128)S(1)}, u32[]{:S(2)}, u32[]{:S(2)}) collective-permute-start(f32[4,256,128]{2,0,1:T(4,128)S(1)} %convolution_add_fusion.2), channel_id=1, source_target_pairs={{0,120},{8,0},{16,8},{24,16},{32,24},{40,32},{48,40},{56,48},{64,5... | collective-permute-start | bytes 1572872 | tf_op jit(solution)/shard_map/while/body/eval_jaxpr/ppermute | solution.py:15
  (45 other events, 4219.5 us)
Sparse Core Ops, SparseCore 0:
  1202.8 149.4 all-reduce.4
where the time goes:
time: 1370 us; the launch traced here: 1360 us
  waiting for transfers between devices  613 us (45%)
  starting transfers between devices  347 us (25%)
  matrix products  315 us (23%)
  blocking collectives  34.1 us (2%)
  other arithmetic  21.3 us (2%)
  between operations  14.8 us (1%)
    ppermute x64, waiting for transfers between devices, shifted(): lax.ppermute(value, axis, [(i, (i + by) % size) for i in range(size)])  499 us
    ppermute x64, starting transfers between devices, shifted(): lax.ppermute(value, axis, [(i, (i + by) % size) for i in range(size)])  347 us
    dot_general x64, matrix products, advance(): updates = jnp.einsum('kab,as->kbs', blocks_now, solved, precision=precise)  163 us
    unnamed x2, waiting for transfers between devices  114 us
    dot_general x64, matrix products, advance(): jnp.einsum('ab,as->bs', inverse_now, source - pending[0], precision=precise)  99 us
    dot_general x64, matrix products, advance(): added_terms = jnp.einsum('kw,kbs->wbs', routing, updates, precision=precise)  51.4 us
    unnamed x1, blocking collectives  34.1 us
  transfers between devices with their start and end apart: 65, of which 65 were waited for; matrix products, arithmetic and copies ran while one was open for 0% of the time, Pallas kernels for 0%

commit v1 on v0

v1 whole, which is shorter than its diff:
```python
import jax
import jax.numpy as jnp
from jax import lax
from jax.experimental import pallas as pl
from jax.experimental.pallas import tpu as pltpu
from jax.sharding import PartitionSpec as P

MESH = pl.DeviceIdType.MESH
F32 = jnp.float32
BF16 = jnp.bfloat16

BS = 256
ROWS = 4
KMAX = 3
COLS = 128
NB = 16
NDIST = 256
SHARE = NDIST // NB
GROUP = 8
PIECES = 4
WIDTH = COLS // PIECES
HALF = COLS // 2


def split(value):
    high = value.astype(BF16)
    return high, (value - high.astype(F32)).astype(BF16)


def dot(a, b):
    return jnp.dot(a, b, preferred_element_type=F32)


def landed(ref, sem):
    pltpu.make_async_copy(ref, ref, sem).wait()


def kernel(
    rhs_ref, lower_ref, col_ref, diag_ref, turn_ref, dist_ref,
    sol_ref, mean_ref,
    diag_high, diag_low, push_out, side_out, push_in, side_in, push_high, push_low,
    zeta, zeta_in, edge_in, edge_out, numer, numer_in, denom, denom_in,
    push_sent, push_got, side_sent, side_got, edge_sent, edge_got,
    zeta_sent, zeta_got, numer_sent, numer_got, denom_sent, denom_got,
):
    b = lax.axis_index("blk")
    s = lax.axis_index("sims")
    y, x = lax.div(b, 4), lax.rem(b, 4)
    core = lax.rem(s, 2)
    plane = s - core

    barrier = pltpu.get_barrier_semaphore()

    def greet(step, carry):
        other = lax.rem(b * 2 + core + step, 32)
        pl.semaphore_signal(
            barrier, inc=1,
            device_id={"blk": lax.div(other, 2), "sims": plane + lax.rem(other, 2)},
            device_id_type=MESH,
        )
        return carry

    lax.fori_loop(1, 32, greet, 0)

    upper = lax.div(y, 2)
    own_y = jnp.where(upper == 1, 2 + core, 1 - core)
    slot = 4 * lax.rem(y, 2) + x

    def prepare(r):
        high, low = split(diag_ref[r])
        diag_high[r] = high
        diag_low[r] = low
        both = jnp.concatenate([high, low], 0)
        for k in range(KMAX):
            l_high, l_low = split(lower_ref[r, k])
            wide = dot(both, l_high)
            push_out[r, k] = wide[:BS] + (wide[BS:] + dot(high, l_low))
        side_out[r, :COLS] = rhs_ref[r].T
        row = 16 * r + b
        masks = []
        for k in (1, 2):
            column = jnp.full((1, BS), col_ref[r, k], jnp.int32)
            for d in (2, 3, 4):
                masks.append(jnp.where((column >= 0) & (column == row - d), 1.0, 0.0).astype(F32))
        masks.append(jnp.zeros((2, BS), F32))
        side_out[r, COLS:] = jnp.concatenate(masks, 0)

    def pieces_of(r):
        to = {"blk": 4 * own_y + r, "sims": plane + 1}
        return (
            (side_out.at[r], side_in.at[slot], side_sent.at[r], side_got.at[slot], to),
            (push_out.at[r], push_in.at[slot], push_sent.at[r], push_got.at[slot], to),
        )

    def stays(r):
        return (core == 1) & (4 * own_y + r == b)

    def hand_over(r):
        @pl.when(stays(r))
        def _():
            for src, dst, _, got, _ in pieces_of(r):
                pltpu.make_async_copy(src, dst, got).start()

        @pl.when(jnp.logical_not(stays(r)))
        def _():
            for src, dst, sent, got, to in pieces_of(r):
                pltpu.make_async_remote_copy(src, dst, sent, got, device_id=to, device_id_type=MESH).start()

    prepare(3)
    pl.semaphore_wait(barrier, 31)
    hand_over(3)

    def prepare_next(step, carry):
        r = 2 - step
        prepare(r)
        hand_over(r)
        return carry

    lax.fori_loop(0, 3, prepare_next, 0)

    def members(r):
        ids = dist_ref[pl.ds(r, 1), :]
        return lax.broadcasted_iota(jnp.int32, (NDIST, BS), 0) == ids

    weight = jnp.zeros((NDIST, BS), F32)
    for r in range(ROWS):
        weight = weight + jnp.where(members(r), turn_ref[r : r + 1, :], 0.0)
    denom[...] = jnp.broadcast_to(jnp.sum(weight, 1, keepdims=True), (NDIST, COLS))
    numer[...] = jnp.zeros_like(numer)

    def exchange(source, target, sent, got):
        def one(step, carry):
            other = lax.rem(b + step, NB)
            pltpu.make_async_remote_copy(
                source.at[pl.ds(SHARE * other, SHARE)], target.at[b], sent.at[other], got.at[b],
                device_id={"blk": other, "sims": s}, device_id_type=MESH,
            ).start()
            return carry

        lax.fori_loop(1, NB, one, 0)
        target[b] = source[pl.ds(pl.multiple_of(SHARE * b, SHARE), SHARE), :]

    def exchanged(source, target, sent, got):
        def one(step, carry):
            other = lax.rem(b + step, NB)
            landed(target.at[other], got.at[other])
            landed(source.at[pl.ds(SHARE * other, SHARE)], sent.at[other])
            return carry

        lax.fori_loop(1, NB, one, 0)

    exchange(denom, denom_in, denom_sent, denom_got)

    def finish(r):
        for part in range(2):
            landed(zeta_in.at[r, pl.ds(HALF * part, HALF)], zeta_got.at[r, part])
        high, low = split(zeta_in[r])
        both = jnp.concatenate([high, low], 0)
        wide = dot(both, diag_high[r])
        field = wide[:COLS] + (wide[COLS:] + dot(high, diag_low[r]))
        sol_ref[r] = field.T
        w_high, w_low = split(field * turn_ref[pl.ds(r, 1), :])
        member = jnp.where(members(r), 1.0, 0.0).astype(BF16)
        contract = (((1,), (1,)), ((), ()))
        numer[...] += lax.dot_general(
            member, w_high, contract, preferred_element_type=F32
        ) + lax.dot_general(member, w_low, contract, preferred_element_type=F32)

    def finish_down(step, carry):
        finish(3 - step)
        return carry

    @pl.when(core == 0)
    def _():
        lax.fori_loop(0, ROWS, finish_down, 0)

    @pl.when(core == 1)
    def _():
        half = lax.div(y, 2)
        part = jnp.where(half == 1, lax.rem(y, 2), 1 - lax.rem(y, 2))
        is_first = (half == 1) & (x == 3)
        is_last = (half == 0) & (x == 0)
        next_b = jnp.where(half == 1, 4 * (1 - part) + x, 4 * (2 + part) + x - 1)

        early = jnp.maximum(2 - x, 0)
        lax.fori_loop(0, early, finish_down, 0)

        def receive(step, carry):
            t = GROUP - 1 - step
            landed(side_in.at[t], side_got.at[t])
            landed(push_in.at[t], push_got.at[t])
            for k in range(KMAX):
                high, low = split(push_in[t, k])
                push_high[t, k] = high
                push_low[t, k] = low
            return carry

        lax.fori_loop(0, GROUP, receive, 0)

        def edge_copies(p):
            to = {"blk": next_b, "sims": s}
            return [
                pltpu.make_async_remote_copy(
                    edge_out.at[p, lo:hi], edge_in.at[p, lo:hi], edge_sent.at[p, n], edge_got.at[p, n],
                    device_id=to, device_id_type=MESH,
                )
                for n, (lo, hi) in enumerate(((0, 1), (1, 4)))
            ]

        def home(t):
            return 4 * (2 * half + lax.div(t, 4)) + lax.rem(t, 4)

        def is_home(t):
            return (part == 1) & (home(t) == b)

        def return_zeta(t, n):
            src = zeta.at[t, pl.ds(HALF * n, HALF)]
            dst = zeta_in.at[x, pl.ds(HALF * n, HALF)]

            @pl.when(is_home(t))
            def _():
                pltpu.make_async_copy(src, dst, zeta_got.at[x, n]).start()

            @pl.when(jnp.logical_not(is_home(t)))
            def _():
                pltpu.make_async_remote_copy(
                    src, dst, zeta_sent.at[t, n], zeta_got.at[x, n],
                    device_id={"blk": home(t), "sims": plane + part}, device_id_type=MESH,
                ).start()

        def piece(p, carry):
            here = pl.ds(pl.multiple_of(WIDTH * p, WIDTH), WIDTH)

            @pl.when(is_first)
            def _():
                edge_in[p] = jnp.zeros((4, WIDTH, BS), F32)

            @pl.when(jnp.logical_not(is_first))
            def _():
                landed(edge_in.at[p, 0:1], edge_got.at[p, 0])
                landed(edge_in.at[p, 1:4], edge_got.at[p, 1])

            pending = [edge_in[p, d] for d in range(4)]
            for t in reversed(range(GROUP)):
                z = side_in[t, here, :] - pending[0]
                zeta[t, here, :] = z
                high, low = split(z)
                both = jnp.concatenate([high, low], 0)
                updates = []
                for k in range(KMAX):
                    wide = dot(both, push_high[t, k])
                    updates.append(wide[:WIDTH] + (wide[WIDTH:] + dot(high, push_low[t, k])))
                moved = [pending[1] + updates[0]]
                for d in range(3):
                    base = pending[2 + d] if d < 2 else jnp.zeros((WIDTH, BS), F32)
                    first = side_in[t, COLS + d : COLS + d + 1, :] > 0.5
                    second = side_in[t, COLS + 3 + d : COLS + 4 + d, :] > 0.5
                    moved.append(
                        base + jnp.where(first, updates[1], jnp.where(second, updates[2], 0.0))
                    )
                pending = moved
            for d in range(4):
                edge_out[p, d] = pending[d]

            @pl.when(jnp.logical_not(is_last))
            def _():
                for copy in edge_copies(p):
                    copy.start()

            @pl.when(lax.rem(p, 2) == 1)
            def _():
                def one(step, c):
                    return_zeta(GROUP - 1 - step, lax.div(p, 2))
                    return c

                lax.fori_loop(0, GROUP, one, 0)

            return carry

        lax.fori_loop(0, PIECES, piece, 0)
        lax.fori_loop(early, ROWS, finish_down, 0)

        @pl.when(jnp.logical_not(is_last))
        def _():
            for p in range(PIECES):
                for copy in edge_copies(p):
                    copy.wait_send()

        def sent_one(step, c):
            t, n = lax.div(step, 2), lax.rem(step, 2)

            @pl.when(jnp.logical_not(is_home(t)))
            def _():
                landed(zeta.at[t, pl.ds(HALF * n, HALF)], zeta_sent.at[t, n])

            return c

        lax.fori_loop(0, 2 * GROUP, sent_one, 0)

    exchange(numer, numer_in, numer_sent, numer_got)

    def handed(r, carry):
        @pl.when(jnp.logical_not(stays(r)))
        def _():
            for src, _, sent, _, _ in pieces_of(r):
                landed(src, sent)

        return carry

    lax.fori_loop(0, ROWS, handed, 0)
    exchanged(denom, denom_in, denom_sent, denom_got)
    exchanged(numer, numer_in, numer_sent, numer_got)
    mean_ref[...] = jnp.sum(numer_in[...], 0) / jnp.sum(denom_in[...], 0)


def body(rhs, lower_blocks, col_index, diag_inverse, turnout, district_of):
    vmem = pl.BlockSpec(memory_space=pltpu.VMEM)
    dma = pltpu.SemaphoreType.DMA
    field, mean = pl.pallas_call(
        kernel,
        out_shape=(
            jax.ShapeDtypeStruct((ROWS, BS, COLS), F32),
            jax.ShapeDtypeStruct((SHARE, COLS), F32),
        ),
        in_specs=[vmem, vmem, pl.BlockSpec(memory_space=pltpu.SMEM), vmem, vmem, vmem],
        out_specs=(vmem, vmem),
        scratch_shapes=[
            pltpu.VMEM((ROWS, BS, BS), BF16),
            pltpu.VMEM((ROWS, BS, BS), BF16),
            pltpu.VMEM((ROWS, KMAX, BS, BS), F32),
            pltpu.VMEM((ROWS, COLS + 8, BS), F32),
            pltpu.VMEM((GROUP, KMAX, BS, BS), F32),
            pltpu.VMEM((GROUP, COLS + 8, BS), F32),
            pltpu.VMEM((GROUP, KMAX, BS, BS), BF16),
            pltpu.VMEM((GROUP, KMAX, BS, BS), BF16),
            pltpu.VMEM((GROUP, COLS, BS), F32),
            pltpu.VMEM((ROWS, COLS, BS), F32),
            pltpu.VMEM((PIECES, 4, WIDTH, BS), F32),
            pltpu.VMEM((PIECES, 4, WIDTH, BS), F32),
            pltpu.VMEM((NDIST, COLS), F32),
            pltpu.VMEM((NB, SHARE, COLS), F32),
            pltpu.VMEM((NDIST, COLS), F32),
            pltpu.VMEM((NB, SHARE, COLS), F32),
            dma((ROWS,)), dma((GROUP,)), dma((ROWS,)), dma((GROUP,)),
            dma((PIECES, 2)), dma((PIECES, 2)),
            dma((GROUP, 2)), dma((ROWS, 2)),
            dma((NB,)), dma((NB,)), dma((NB,)), dma((NB,)),
        ],
        name="back_substitution",
        compiler_params=pltpu.CompilerParams(
            collective_id=0, has_side_effects=True, vmem_limit_bytes=48 * 1024 * 1024
        ),
    )(
        rhs[:, 0], lower_blocks[:, 0], col_index[:, 0], diag_inverse[:, 0], turnout[:, 0], district_of[:, 0]
    )
    return field[:, None], mean


def solution(mesh):
    placed = (
        P(None, "blk", None, "sims"),
        P(None, "blk", None, None, None),
        P(None, "blk", None),
        P(None, "blk", None, None),
        P(None, "blk", None),
        P(None, "blk", None),
    )
    return jax.shard_map(
        body,
        mesh=mesh,
        in_specs=placed,
        out_specs=(P(None, "blk", None, "sims"), P("blk", "sims")),
        check_vma=False,
    )
```

time: 1370 us -> 115 us (0.08)
  waiting for transfers between devices: 613 us -> 0 us
  starting transfers between devices: 347 us -> 0 us
  matrix products: 315 us -> 0 us
  Pallas kernels: 0 us -> 107 us
  blocking collectives: 34.1 us -> 0 us
  other arithmetic: 21.3 us -> 0 us
  between operations: 14.8 us -> 0.64 us
    ppermute x64 -> x0, waiting for transfers between devices: 499 us -> none  [shifted(): lax.ppermute(value, axis, [(i, (i + by) % size) for i in range(size)])]
    ppermute x64 -> x0, starting transfers between devices: 347 us -> none  [shifted(): lax.ppermute(value, axis, [(i, (i + by) % size) for i in range(size)])]
    dot_general x194 -> x0, matrix products: 315 us -> none  [the longest x64 163 us: advance(): updates = jnp.einsum('kab,as->kbs', blocks_now, solved, precision=precise)]
    unnamed x2 -> x0, waiting for transfers between devices: 114 us -> none
    pallas_call x0 -> x1, Pallas kernels: none -> 107 us  [body(): pl.pallas_call(kernel, out_shape=(jax.ShapeDtypeStruct((ROWS, BS, COLS),...]
    unnamed x1 -> x0, blocking collectives: 34.1 us -> none
  transfers between devices with their start and end apart: 65 -> 0, of which waited for: 65 -> 0; matrix products, arithmetic and copies ran while one was open for 0% -> 0% of each run, Pallas kernels for 0% -> 0%
where the time goes in v1:
time: 115 us
  Pallas kernels  107 us (93%)
  local copies, waits for them, and re-layouts  7.69 us (7%)
    pallas_call x1, Pallas kernels, body(): pl.pallas_call(kernel, out_shape=(jax.ShapeDtypeStruct((ROWS, BS, COLS),...  107 us
    unnamed x11, local copies, waits for them, and re-layouts  7.69 us

profile of v1, /device:TPU:1, one launch (start us, length us, event | category | flops | bytes accessed | tf_op | source)
XLA Modules:
  0.0 114.8 jit_solution(12210135964270855379)
XLA Ops:
  0.6 0.8 copy.8
  1.4 0.7 copy.15
  2.1 0.7 copy.14
  2.8 0.0 copy-start
  2.8 1.9 %copy-done = f32[4,1,3,256,256]{4,3,2,1,0:T(8,128)S(1)} copy-done((f32[4,1,3,256,256]{4,3,2,1,0:T(8,128)S(1)}, f32[4,1,3,256,256]{4,3,2,1,0:T(8,128)}, u32[]{:S(2)}) %copy-start) | copy-done | bytes 3145752
  4.7 0.0 copy-start.1
  4.7 1.2 %copy-done.1 = f32[4,1,256,256]{3,2,1,0:T(8,128)S(1)} copy-done((f32[4,1,256,256]{3,2,1,0:T(8,128)S(1)}, f32[4,1,256,256]{3,2,1,0:T(8,128)}, u32[]{:S(2)}) %copy-start.1) | copy-done | bytes 1048600
  5.9 0.0 copy-start.2
  5.9 1.0 copy-done.2
  6.9 106.5 %back_substitution.1 = (f32[4,256,128]{2,1,0:T(8,128)S(1)}, f32[16,128]{1,0:T(8,128)S(1)}) custom-call(f32[4,256,128]{2,1,0:T(8,128)S(1)} %bitcast.15, f32[4,3,256,256]{3,2,1,0:T(8,128)S(1)} %bitcast.13, s32[4,3]{1,0:T(4,128)S(1)} %bitcast.19, f32[4,256,256]{2,1,0:T(8,128)S(1)} %bitcast.14, f32[4,256]{1,0:T(4,128)S(1)} %bitcast.17, s32[4,256]{1,0:T(4,128)S(1)} %bitcast.18), custom_call_target="tpu_custom_call" | custom-call | tf_op jit(solution)/shard_map/back_substitution/pallas_call | solution.py:319
  113.5 0.8 copy.18
  114.3 0.6 copy.19
Async XLA Ops:
  2.8 1.9 %copy-start = (f32[4,1,3,256,256]{4,3,2,1,0:T(8,128)S(1)}, f32[4,1,3,256,256]{4,3,2,1,0:T(8,128)}, u32[]{:S(2)}) copy-start(f32[4,1,3,256,256]{4,3,2,1,0:T(8,128)} %param.7) | copy-start | bytes 9437188
  4.7 1.2 %copy-start.1 = (f32[4,1,256,256]{3,2,1,0:T(8,128)S(1)}, f32[4,1,256,256]{3,2,1,0:T(8,128)}, u32[]{:S(2)}) copy-start(f32[4,1,256,256]{3,2,1,0:T(8,128)} %param.9) | copy-start | bytes 3145732
  5.9 1.0 copy-start.2

commit v2 on v1

v2 whole, which is shorter than its diff:
```python
import jax
import jax.numpy as jnp
from jax import lax
from jax.experimental import pallas as pl
from jax.experimental.pallas import tpu as pltpu
from jax.sharding import PartitionSpec as P

MESH = pl.DeviceIdType.MESH
F32 = jnp.float32
BF16 = jnp.bfloat16

BS = 256
ROWS = 4
KMAX = 3
COLS = 128
NB = 16
NDIST = 256
SHARE = NDIST // NB
GROUP = 8
PIECES = 4
WIDTH = COLS // PIECES
HALF = COLS // 2


def split(value):
    high = value.astype(BF16)
    return high, (value - high.astype(F32)).astype(BF16)


def dot(a, b):
    return jnp.dot(a, b, preferred_element_type=F32)


def landed(ref, sem):
    pltpu.make_async_copy(ref, ref, sem).wait()


def in_hbm(array):
    return pltpu.with_memory_space_constraint(array, pltpu.HBM)


def kernel(
    rhs_hbm, lower_hbm, col_ref, diag_hbm, turn_ref, dist_ref,
    sol_ref, mean_ref,
    rhs_ref, lower_ref, diag_ref,
    diag_high, diag_low, push_out, side_out, push_in, side_in, push_high, push_low,
    zeta, zeta_in, edge_in, edge_out, numer, numer_in, denom, denom_in,
    read_got, push_sent, push_got, pass_sent, pass_got, side_sent, side_got, edge_sent, edge_got,
    zeta_sent, zeta_got, numer_sent, numer_got, denom_sent, denom_got,
):
    b = lax.axis_index("blk")
    s = lax.axis_index("sims")
    y, x = lax.div(b, 4), lax.rem(b, 4)
    core = lax.rem(s, 2)
    plane = s - core
    z_here = lax.div(s, 2)
    mine = pl.multiple_of(128 * lax.rem(z_here, 2), 128)

    def reads(r):
        return (
            pltpu.make_async_copy(diag_hbm.at[r, 0], diag_ref.at[r], read_got.at[r, 0]),
            pltpu.make_async_copy(lower_hbm.at[r, 0], lower_ref.at[r], read_got.at[r, 1]),
            pltpu.make_async_copy(rhs_hbm.at[r, 0], rhs_ref.at[r], read_got.at[r, 2]),
        )

    def start_reads(step, carry):
        for copy in reads(3 - step):
            copy.start()
        return carry

    lax.fori_loop(0, ROWS, start_reads, 0)

    barrier = pltpu.get_barrier_semaphore()

    def hail(other_blk, other_sims):
        pl.semaphore_signal(barrier, inc=1, device_id={"blk": other_blk, "sims": other_sims}, device_id_type=MESH)

    upper = lax.div(y, 2)
    lane = jnp.where(upper == 1, lax.rem(y, 2), 1 - lax.rem(y, 2))

    def greet(step, carry):
        hail(lax.rem(b + step, NB), s)
        return carry

    lax.fori_loop(1, NB, greet, 0)

    @pl.when(core == 0)
    def _():
        for r in range(ROWS):
            hail(4 * jnp.where(upper == 1, 2, 1) + r, plane + 1)

    @pl.when((core == 1) & (lane == 0))
    def _():
        for t in range(GROUP):
            hail(8 * upper + t, plane)

    above = plane + core + 2 - 8 * lax.div(plane + 2, 8)
    below = lax.rem(plane + 6, 8) + core
    for other in (above, below):
        pl.semaphore_signal(barrier, inc=1, device_id={"blk": b, "sims": other}, device_id_type=MESH)

    upper = lax.div(y, 2)
    own_y = jnp.where(upper == 1, 2 + core, 1 - core)
    slot = 4 * lax.rem(y, 2) + x

    def prepare_side(r):
        for copy in reads(r):
            copy.wait()
        high, low = split(diag_ref[r])
        diag_high[r] = high
        diag_low[r] = low
        side_out[r, :COLS] = rhs_ref[r].T
        row = 16 * r + b
        masks = []
        for k in (1, 2):
            column = jnp.full((1, BS), col_ref[k, 0, r], jnp.int32)
            for d in (2, 3, 4):
                masks.append(jnp.where((column >= 0) & (column == row - d), 1.0, 0.0).astype(F32))
        masks.append(jnp.zeros((2, BS), F32))
        side_out[r, COLS:] = jnp.concatenate(masks, 0)

    def prepare(r, k):
        high, low = diag_high[r, pl.ds(mine, 128), :], diag_low[r, pl.ds(mine, 128), :]
        both = jnp.concatenate([high, low], 0)
        l_high, l_low = split(lower_ref[r, k])
        wide = dot(both, l_high)
        push_out[r, k] = wide[:128] + (wide[128:] + dot(high, l_low))

    def side_of(r):
        return side_out.at[r], side_in.at[slot], side_sent.at[r], side_got.at[slot]

    def push_of(r, k):
        return push_out.at[r, k], push_in.at[slot, k, pl.ds(mine, 128)], push_sent.at[r, k], push_got.at[slot, k]

    def stays(r):
        return (core == 1) & (4 * own_y + r == b)

    def hand_over(r, what):
        src, dst, sent, got = what

        @pl.when(stays(r))
        def _():
            pltpu.make_async_copy(src, dst, got).start()

        @pl.when(jnp.logical_not(stays(r)))
        def _():
            to = {"blk": 4 * own_y + r, "sims": plane + 1}
            pltpu.make_async_remote_copy(src, dst, sent, got, device_id=to, device_id_type=MESH).start()

    def quarter(t, k, n):
        where = push_in.at[t, k, pl.ds(mine + 64 * n, 64)]
        return pltpu.make_async_remote_copy(
            where, where, pass_sent.at[t, k, n], pass_got.at[t, k, n],
            device_id={"blk": b, "sims": (above, below)[n]}, device_id_type=MESH,
        )

    def keep(t, k, start):
        rows = pl.ds(start, 128)
        high, low = split(push_in[t, k, rows, :])
        push_high[t, k, rows, :] = high
        push_low[t, k, rows, :] = low

    def forward(step, carry):
        k, t = lax.div(step, GROUP), GROUP - 1 - lax.rem(step, GROUP)
        landed(push_in.at[t, k, pl.ds(mine, 128)], push_got.at[t, k])
        for n in range(2):
            quarter(t, k, n).start()
        keep(t, k, mine)
        return carry

    def forward_all(k):
        def one(step, carry):
            forward(k * GROUP + step, 0)
            return carry

        lax.fori_loop(0, GROUP, one, 0)

    def sent(r, refs):
        @pl.when(jnp.logical_not(stays(r)))
        def _():
            for ref, sem in refs:
                landed(ref, sem)

    def sent_push(k):
        def one(r, carry):
            sent(r, [(push_out.at[r, k], push_sent.at[r, k])])
            return carry

        lax.fori_loop(0, ROWS, one, 0)

    def prepare_all(k):
        def one(step, carry):
            r = 3 - step
            prepare(r, k)
            hand_over(r, push_of(r, k))
            return carry

        lax.fori_loop(0, ROWS, one, 0)

    prepare_side(3)
    prepare(3, 0)
    pl.semaphore_wait(barrier, NB + 1 + jnp.where(core == 0, ROWS, jnp.where(lane == 0, GROUP, 0)))
    hand_over(3, push_of(3, 0))

    def prepare_first(step, carry):
        r = 2 - step
        prepare_side(r)
        prepare(r, 0)
        hand_over(r, push_of(r, 0))
        return carry

    lax.fori_loop(0, 3, prepare_first, 0)
    prepare_all(1)

    @pl.when(core == 1)
    def _():
        forward_all(0)


    prepare_all(2)
    hand_over(3, side_of(3))

    @pl.when(core == 1)
    def _():
        forward_all(1)

    sent_push(0)
    sent_push(1)
    sent_push(2)
    for r in (2, 1, 0):
        hand_over(r, side_of(r))

    @pl.when(core == 1)
    def _():
        forward_all(2)

    def members(r):
        ids = dist_ref[r]
        return lax.broadcasted_iota(jnp.int32, (NDIST, BS), 0) == ids

    numer[...] = jnp.zeros_like(numer)

    def exchange(source, target, sent, got):
        def one(step, carry):
            other = lax.rem(b + step, NB)
            pltpu.make_async_remote_copy(
                source.at[pl.ds(SHARE * other, SHARE)], target.at[b], sent.at[other], got.at[b],
                device_id={"blk": other, "sims": s}, device_id_type=MESH,
            ).start()
            return carry

        lax.fori_loop(1, NB, one, 0)
        target[b] = source[pl.ds(pl.multiple_of(SHARE * b, SHARE), SHARE), :]

    def exchanged(source, target, sent, got):
        def one(step, carry):
            other = lax.rem(b + step, NB)
            landed(target.at[other], got.at[other])
            landed(source.at[pl.ds(SHARE * other, SHARE)], sent.at[other])
            return carry

        lax.fori_loop(1, NB, one, 0)

    def share_weights():
        weight = jnp.zeros((NDIST, BS), F32)
        for r in range(ROWS):
            weight = weight + jnp.where(members(r), turn_ref[r], 0.0)
        denom[...] = jnp.broadcast_to(jnp.sum(weight, 1, keepdims=True), (NDIST, COLS))
        exchange(denom, denom_in, denom_sent, denom_got)

    @pl.when((core == 0) | (x < 3))
    def _():
        share_weights()

    def finish(r):
        for part in range(2):
            landed(zeta_in.at[r, pl.ds(HALF * part, HALF)], zeta_got.at[r, part])
        high, low = split(zeta_in[r])
        both = jnp.concatenate([high, low], 0)
        wide = dot(both, diag_high[r])
        field = wide[:COLS] + (wide[COLS:] + dot(high, diag_low[r]))
        sol_ref[r] = field.T
        w_high, w_low = split(field * turn_ref[r])
        member = jnp.where(members(r), 1.0, 0.0).astype(BF16)
        contract = (((1,), (1,)), ((), ()))
        numer[...] += lax.dot_general(
            member, w_high, contract, preferred_element_type=F32
        ) + lax.dot_general(member, w_low, contract, preferred_element_type=F32)

    def finish_down(step, carry):
        finish(3 - step)
        return carry

    @pl.when(core == 0)
    def _():
        lax.fori_loop(0, ROWS, finish_down, 0)

    @pl.when(core == 1)
    def _():
        half = lax.div(y, 2)
        part = jnp.where(half == 1, lax.rem(y, 2), 1 - lax.rem(y, 2))
        is_first = (half == 1) & (x == 3)
        is_last = (half == 0) & (x == 0)
        next_b = jnp.where(half == 1, 4 * (1 - part) + x, 4 * (2 + part) + x - 1)

        early = jnp.maximum(2 - x, 0)
        theirs = pl.multiple_of(128 - mine, 128)

        def receive(step, carry):
            k, t = lax.div(step, GROUP), GROUP - 1 - lax.rem(step, GROUP)
            for n in range(2):
                landed(push_in.at[t, k, pl.ds(theirs + 64 * n, 64)], pass_got.at[t, k, n])
            keep(t, k, theirs)
            return carry

        lax.fori_loop(0, KMAX * GROUP, receive, 0)

        def receive_side(t, carry):
            landed(side_in.at[t], side_got.at[t])
            return carry

        lax.fori_loop(0, GROUP, receive_side, 0)

        def edge_copy(p, d):
            return pltpu.make_async_remote_copy(
                edge_out.at[p, d], edge_in.at[p, d], edge_sent.at[p, d], edge_got.at[p, d],
                device_id={"blk": next_b, "sims": s}, device_id_type=MESH,
            )

        @pl.when(is_first)
        def _():
            edge_out[...] = jnp.zeros_like(edge_out)
            for p in range(PIECES):
                for d in range(4):
                    pltpu.make_async_copy(edge_out.at[p, d], edge_in.at[p, d], edge_got.at[p, d]).start()

        def home(t):
            return 4 * (2 * half + lax.div(t, 4)) + lax.rem(t, 4)

        def is_home(t):
            return (part == 1) & (home(t) == b)

        def return_zeta(t, n):
            src = zeta.at[t, pl.ds(HALF * n, HALF)]
            dst = zeta_in.at[x, pl.ds(HALF * n, HALF)]

            @pl.when(is_home(t))
            def _():
                pltpu.make_async_copy(src, dst, zeta_got.at[x, n]).start()

            @pl.when(jnp.logical_not(is_home(t)))
            def _():
                pltpu.make_async_remote_copy(
                    src, dst, zeta_sent.at[t, n], zeta_got.at[x, n],
                    device_id={"blk": home(t), "sims": plane + part}, device_id_type=MESH,
                ).start()

        def piece(p, carry):
            here = pl.ds(pl.multiple_of(WIDTH * p, WIDTH), WIDTH)

            def far(t, both, high, pending):
                updates = []
                for k in (1, 2):
                    wide = dot(both, push_high[t, k])
                    updates.append(wide[:WIDTH] + (wide[WIDTH:] + dot(high, push_low[t, k])))
                for d in range(3):
                    first = side_in[t, COLS + d : COLS + d + 1, :] > 0.5
                    second = side_in[t, COLS + 3 + d : COLS + 4 + d, :] > 0.5
                    update = jnp.where(first, updates[0], jnp.where(second, updates[1], 0.0))
                    row = t - 2 - d
                    pending[row] = pending[row] + update if row in pending else update

            pending = {}
            for t in reversed(range(GROUP)):
                d = GROUP - 1 - t
                if d < 4:
                    landed(edge_in.at[p, d], edge_got.at[p, d])
                    edge = edge_in[p, d]
                    pending[t] = pending[t] + edge if t in pending else edge
                z = side_in[t, here, :] - pending[t]
                zeta[t, here, :] = z
                high, low = split(z)
                both = jnp.concatenate([high, low], 0)
                wide = dot(both, push_high[t, 0])
                low_part = dot(high, push_low[t, 0])
                update = wide[:WIDTH] + (wide[WIDTH:] + low_part)
                if t > 0:
                    far(t, both, high, pending)
                pending[t - 1] = pending[t - 1] + update if t - 1 in pending else update
            edge_out[p, 0] = pending[-1]

            @pl.when(jnp.logical_not(is_last))
            def _():
                edge_copy(p, 0).start()

            far(0, both, high, pending)
            for d in range(1, 4):
                edge_out[p, d] = pending[-1 - d]

            @pl.when(jnp.logical_not(is_last))
            def _():
                for d in range(1, 4):
                    edge_copy(p, d).start()

            @pl.when(lax.rem(p, PIECES // 2) == PIECES // 2 - 1)
            def _():
                def one(step, c):
                    return_zeta(GROUP - 1 - step, lax.div(p, PIECES // 2))
                    return c

                lax.fori_loop(0, GROUP, one, 0)

            return carry

        lax.fori_loop(0, early, finish_down, 0)
        lax.fori_loop(0, PIECES, piece, 0)

        @pl.when(x == 3)
        def _():
            share_weights()

        lax.fori_loop(early, ROWS, finish_down, 0)

        @pl.when(jnp.logical_not(is_last))
        def _():
            for p in range(PIECES):
                for d in range(4):
                    edge_copy(p, d).wait_send()

        def sent_one(step, c):
            t, n = lax.div(step, 2), lax.rem(step, 2)

            @pl.when(jnp.logical_not(is_home(t)))
            def _():
                landed(zeta.at[t, pl.ds(HALF * n, HALF)], zeta_sent.at[t, n])

            return c

        lax.fori_loop(0, 2 * GROUP, sent_one, 0)

        def passed(t, c):
            for k in range(KMAX):
                for n in range(2):
                    quarter(t, k, n).wait_send()
            return c

        lax.fori_loop(0, GROUP, passed, 0)

    exchange(numer, numer_in, numer_sent, numer_got)

    def sent_side(r, carry):
        sent(r, [(side_out.at[r], side_sent.at[r])])
        return carry

    lax.fori_loop(0, ROWS, sent_side, 0)
    exchanged(denom, denom_in, denom_sent, denom_got)
    exchanged(numer, numer_in, numer_sent, numer_got)
    mean_ref[...] = jnp.sum(numer_in[...], 0) / jnp.sum(denom_in[...], 0)


def body(rhs, lower_blocks, col_index, diag_inverse, turnout, district_of):
    vmem = pl.BlockSpec(memory_space=pltpu.VMEM)
    hbm = pl.BlockSpec(memory_space=pltpu.HBM)
    dma = pltpu.SemaphoreType.DMA
    field, mean = pl.pallas_call(
        kernel,
        out_shape=(
            jax.ShapeDtypeStruct((ROWS, BS, COLS), F32),
            jax.ShapeDtypeStruct((SHARE, COLS), F32),
        ),
        in_specs=[hbm, hbm, pl.BlockSpec(memory_space=pltpu.SMEM), hbm, vmem, vmem],
        out_specs=(vmem, vmem),
        scratch_shapes=[
            pltpu.VMEM((ROWS, BS, COLS), F32),
            pltpu.VMEM((ROWS, KMAX, BS, BS), F32),
            pltpu.VMEM((ROWS, BS, BS), F32),
            pltpu.VMEM((ROWS, BS, BS), BF16),
            pltpu.VMEM((ROWS, BS, BS), BF16),
            pltpu.VMEM((ROWS, KMAX, BS // 2, BS), F32),
            pltpu.VMEM((ROWS, COLS + 8, BS), F32),
            pltpu.VMEM((GROUP, KMAX, BS, BS), F32),
            pltpu.VMEM((GROUP, COLS + 8, BS), F32),
            pltpu.VMEM((GROUP, KMAX, BS, BS), BF16),
            pltpu.VMEM((GROUP, KMAX, BS, BS), BF16),
            pltpu.VMEM((GROUP, COLS, BS), F32),
            pltpu.VMEM((ROWS, COLS, BS), F32),
            pltpu.VMEM((PIECES, 4, WIDTH, BS), F32),
            pltpu.VMEM((PIECES, 4, WIDTH, BS), F32),
            pltpu.VMEM((NDIST, COLS), F32),
            pltpu.VMEM((NB, SHARE, COLS), F32),
            pltpu.VMEM((NDIST, COLS), F32),
            pltpu.VMEM((NB, SHARE, COLS), F32),
            dma((ROWS, 3)), dma((ROWS, KMAX)), dma((GROUP, KMAX)), dma((GROUP, KMAX, 2)), dma((GROUP, KMAX, 2)),
            dma((ROWS,)), dma((GROUP,)), dma((PIECES, 4)), dma((PIECES, 4)),
            dma((GROUP, 2)), dma((ROWS, 2)),
            dma((NB,)), dma((NB,)), dma((NB,)), dma((NB,)),
        ],
        name="back_substitution",
        compiler_params=pltpu.CompilerParams(
            collective_id=0, has_side_effects=True, vmem_limit_bytes=48 * 1024 * 1024
        ),
    )(
        in_hbm(rhs), in_hbm(lower_blocks), jnp.transpose(col_index, (2, 1, 0)), in_hbm(diag_inverse),
        turnout, district_of,
    )
    return field[:, None], mean


def solution(mesh):
    placed = (
        P(None, "blk", None, "sims"),
        P(None, "blk", None, None, None),
        P(None, "blk", None),
        P(None, "blk", None, None),
        P(None, "blk", None),
        P(None, "blk", None),
    )
    return jax.shard_map(
        body,
        mesh=mesh,
        in_specs=placed,
        out_specs=(P(None, "blk", None, "sims"), P("blk", "sims")),
        check_vma=False,
    )
```

time: 115 us -> 96.9 us (0.84)
  Pallas kernels: 107 us -> 92.6 us
  local copies, waits for them, and re-layouts: 7.69 us -> 3.44 us
    pallas_call x1, Pallas kernels: 107 us -> 92.6 us  [body(): pl.pallas_call(kernel, out_shape=(jax.ShapeDtypeStruct((ROWS, BS, COLS),...]
    unnamed x11 -> x8, local copies, waits for them, and re-layouts: 7.69 us -> 3.44 us
where the time goes in v2:
time: 96.9 us; the launch traced here: 96.7 us
  Pallas kernels  92.6 us (96%)
  local copies, waits for them, and re-layouts  3.44 us (4%)
    pallas_call x1, Pallas kernels, body(): pl.pallas_call(kernel, out_shape=(jax.ShapeDtypeStruct((ROWS, BS, COLS),...  92.6 us
    unnamed x8, local copies, waits for them, and re-layouts  3.44 us

profile of v2, /device:TPU:1, one launch (start us, length us, event | category | flops | bytes accessed | tf_op | source)
XLA Modules:
  0.0 96.7 jit_solution(13726154594428197209)
XLA Ops:
  0.6 0.0 copy-start
  0.6 0.7 copy-done
  1.3 0.0 copy-start.1
  1.3 0.7 copy-done.1
  2.0 0.0 copy-start.2
  2.0 0.7 copy-done.2
  2.7 92.6 %back_substitution.1 = (f32[4,256,128]{2,1,0:T(8,128)S(1)}, f32[16,128]{1,0:T(8,128)S(1)}) custom-call(f32[4,1,256,128]{3,2,1,0:T(8,128)} %rhs_hbm.1, f32[4,1,3,256,256]{4,3,2,1,0:T(8,128)} %lower_hbm.1, s32[3,1,4]{2,1,0:T(1,128)S(1)} %bitcast.5, f32[4,1,256,256]{3,2,1,0:T(8,128)} %diag_hbm.1, f32[4,1,256]{2,1,0:T(1,128)S(1)} %copy-done, ...), custom_call_target="tpu_custom_call" | custom-call | tf_op jit(solution)/shard_map/back_substitution/pallas_call | solution.py:465
  95.3 0.8 copy.11
  96.1 0.6 copy.12
Async XLA Ops:
  0.6 0.7 copy-start
  1.3 0.7 copy-start.1
  2.0 0.7 copy-start.2

commit v3 on v2

--- a/solution.py
+++ b/solution.py
@@ -19,7 +19,6 @@
 GROUP = 8
 PIECES = 4
 WIDTH = COLS // PIECES
-HALF = COLS // 2
 
 
 def split(value):
@@ -40,12 +39,12 @@
 
 
 def kernel(
-    rhs_hbm, lower_hbm, col_ref, diag_hbm, turn_ref, dist_ref,
+    rhs_hbm, lower_hbm, col_ref, diag_hbm, turn_hbm, dist_hbm,
     sol_ref, mean_ref,
-    rhs_ref, lower_ref, diag_ref,
-    diag_high, diag_low, push_out, side_out, push_in, side_in, push_high, push_low,
+    rhs_ref, lower_ref, diag_ref, turn_ref, dist_ref,
+    diag_high, diag_low, push_out, side_out, side_twin, push_in, side_in, push_high, push_low,
     zeta, zeta_in, edge_in, edge_out, numer, numer_in, denom, denom_in,
-    read_got, push_sent, push_got, pass_sent, pass_got, side_sent, side_got, edge_sent, edge_got,
+    read_got, small_got, push_sent, push_got, pass_sent, pass_got, twin_sent, twin_got, side_sent, side_got, edge_sent, edge_got,
     zeta_sent, zeta_got, numer_sent, numer_got, denom_sent, denom_got,
 ):
     b = lax.axis_index("blk")
@@ -69,6 +68,12 @@
         return carry
 
     lax.fori_loop(0, ROWS, start_reads, 0)
+    small = (
+        pltpu.make_async_copy(turn_hbm, turn_ref, small_got.at[0]),
+        pltpu.make_async_copy(dist_hbm, dist_ref, small_got.at[1]),
+    )
+    for copy in small:
+        copy.start()
 
     barrier = pltpu.get_barrier_semaphore()
 
@@ -87,9 +92,10 @@
     @pl.when(core == 0)
     def _():
         for r in range(ROWS):
-            hail(4 * jnp.where(upper == 1, 2, 1) + r, plane + 1)
-
-    @pl.when((core == 1) & (lane == 0))
+            for there in (0, 1):
+                hail(4 * jnp.where(upper == 1, 2 + there, 1 - there) + r, plane + 1)
+
+    @pl.when(core == 1)
     def _():
         for t in range(GROUP):
             hail(8 * upper + t, plane)
@@ -126,26 +132,37 @@
         wide = dot(both, l_high)
         push_out[r, k] = wide[:128] + (wide[128:] + dot(high, l_low))
 
-    def side_of(r):
-        return side_out.at[r], side_in.at[slot], side_sent.at[r], side_got.at[slot]
-
-    def push_of(r, k):
-        return push_out.at[r, k], push_in.at[slot, k, pl.ds(mine, 128)], push_sent.at[r, k], push_got.at[slot, k]
-
-    def stays(r):
-        return (core == 1) & (4 * own_y + r == b)
-
-    def hand_over(r, what):
-        src, dst, sent, got = what
-
-        @pl.when(stays(r))
-        def _():
-            pltpu.make_async_copy(src, dst, got).start()
-
-        @pl.when(jnp.logical_not(stays(r)))
-        def _():
-            to = {"blk": 4 * own_y + r, "sims": plane + 1}
-            pltpu.make_async_remote_copy(src, dst, sent, got, device_id=to, device_id_type=MESH).start()
+    def owner_of(r, there):
+        return {"blk": 4 * jnp.where(upper == 1, 2 + there, 1 - there) + r, "sims": plane + 1}
+
+    def twin_copy(r):
+        return pltpu.make_async_remote_copy(
+            side_out.at[r], side_twin.at[r], twin_sent.at[r], twin_got.at[r],
+            device_id={"blk": b, "sims": plane}, device_id_type=MESH,
+        )
+
+    def side_copies(r):
+        return [
+            pltpu.make_async_remote_copy(
+                (side_out, side_twin)[there].at[r], side_in.at[slot], side_sent.at[r, there], side_got.at[slot],
+                device_id=owner_of(r, there), device_id_type=MESH,
+            )
+            for there in (0, 1)
+        ]
+
+    def send_side(r):
+        landed(side_twin.at[r], twin_got.at[r])
+        for copy in side_copies(r):
+            copy.start()
+
+    def push_copies(r, k):
+        return [
+            pltpu.make_async_remote_copy(
+                push_out.at[r, k], push_in.at[slot, k, pl.ds(mine, 128)], push_sent.at[r, k, there], push_got.at[slot, k],
+                device_id=owner_of(r, there), device_id_type=MESH,
+            )
+            for there in (0, 1)
+        ]
 
     def quarter(t, k, n):
         where = push_in.at[t, k, pl.ds(mine + 64 * n, 64)]
@@ -168,6 +185,18 @@
         keep(t, k, mine)
         return carry
 
+    def receive_all(k):
+        theirs = pl.multiple_of(128 - mine, 128)
+
+        def one(step, carry):
+            t = GROUP - 1 - step
+            for n in range(2):
+                landed(push_in.at[t, k, pl.ds(theirs + 64 * n, 64)], pass_got.at[t, k, n])
+            keep(t, k, theirs)
+            return carry
+
+        lax.fori_loop(0, GROUP, one, 0)
+
     def forward_all(k):
         def one(step, carry):
             forward(k * GROUP + step, 0)
@@ -175,64 +204,74 @@
 
         lax.fori_loop(0, GROUP, one, 0)
 
-    def sent(r, refs):
-        @pl.when(jnp.logical_not(stays(r)))
-        def _():
-            for ref, sem in refs:
-                landed(ref, sem)
-
     def sent_push(k):
         def one(r, carry):
-            sent(r, [(push_out.at[r, k], push_sent.at[r, k])])
+            for copy in push_copies(r, k):
+                copy.wait_send()
             return carry
 
         lax.fori_loop(0, ROWS, one, 0)
 
-    def prepare_all(k):
+    def push_all(k):
         def one(step, carry):
             r = 3 - step
             prepare(r, k)
-            hand_over(r, push_of(r, k))
+            for copy in push_copies(r, k):
+                copy.start()
             return carry
 
         lax.fori_loop(0, ROWS, one, 0)
 
-    prepare_side(3)
-    prepare(3, 0)
-    pl.semaphore_wait(barrier, NB + 1 + jnp.where(core == 0, ROWS, jnp.where(lane == 0, GROUP, 0)))
-    hand_over(3, push_of(3, 0))
-
-    def prepare_first(step, carry):
-        r = 2 - step
-        prepare_side(r)
-        prepare(r, 0)
-        hand_over(r, push_of(r, 0))
+    def prepare_sides(step, carry):
+        prepare_side(3 - step)
         return carry
 
-    lax.fori_loop(0, 3, prepare_first, 0)
-    prepare_all(1)
+    lax.fori_loop(0, 1, prepare_sides, 0)
+
+    @pl.when(core == 0)
+    def _():
+        prepare(3, 0)
+
+    pl.semaphore_wait(barrier, NB + 1 + 2 * ROWS)
+
+    @pl.when(core == 0)
+    def _():
+        for copy in push_copies(3, 0):
+            copy.start()
+
+    lax.fori_loop(1, ROWS, prepare_sides, 0)
+
+    @pl.when(core == 0)
+    def _():
+        def first(step, carry):
+            r = 2 - step
+            prepare(r, 0)
+            for copy in push_copies(r, 0):
+                copy.start()
+            return carry
+
+        lax.fori_loop(0, 3, first, 0)
+        push_all(1)
+        push_all(2)
+        send_side(3)
+        for k in range(KMAX):
+            sent_push(k)
+        for r in (2, 1, 0):
+            send_side(r)
 
     @pl.when(core == 1)
     def _():
+        for r in range(ROWS):
+            twin_copy(r).start()
         forward_all(0)
-
-
-    prepare_all(2)
-    hand_over(3, side_of(3))
-
-    @pl.when(core == 1)
-    def _():
         forward_all(1)
-
-    sent_push(0)
-    sent_push(1)
-    sent_push(2)
-    for r in (2, 1, 0):
-        hand_over(r, side_of(r))
-
-    @pl.when(core == 1)
-    def _():
+        receive_all(0)
         forward_all(2)
+        receive_all(1)
+        receive_all(2)
+
+    for copy in small:
+        copy.wait()
 
     def members(r):
         ids = dist_ref[r]
@@ -249,7 +288,7 @@
             ).start()
             return carry
 
-        lax.fori_loop(1, NB, one, 0)
+        lax.fori_loop(1, NB, one, 0, unroll=True)
         target[b] = source[pl.ds(pl.multiple_of(SHARE * b, SHARE), SHARE), :]
 
     def exchanged(source, target, sent, got):
@@ -259,7 +298,7 @@
             landed(source.at[pl.ds(SHARE * other, SHARE)], sent.at[other])
             return carry
 
-        lax.fori_loop(1, NB, one, 0)
+        lax.fori_loop(1, NB, one, 0, unroll=True)
 
     def share_weights():
         weight = jnp.zeros((NDIST, BS), F32)
@@ -273,8 +312,7 @@
         share_weights()
 
     def finish(r):
-        for part in range(2):
-            landed(zeta_in.at[r, pl.ds(HALF * part, HALF)], zeta_got.at[r, part])
+        landed(zeta_in.at[r], zeta_got.at[r])
         high, low = split(zeta_in[r])
         both = jnp.concatenate([high, low], 0)
         wide = dot(both, diag_high[r])
@@ -304,17 +342,6 @@
         next_b = jnp.where(half == 1, 4 * (1 - part) + x, 4 * (2 + part) + x - 1)
 
         early = jnp.maximum(2 - x, 0)
-        theirs = pl.multiple_of(128 - mine, 128)
-
-        def receive(step, carry):
-            k, t = lax.div(step, GROUP), GROUP - 1 - lax.rem(step, GROUP)
-            for n in range(2):
-                landed(push_in.at[t, k, pl.ds(theirs + 64 * n, 64)], pass_got.at[t, k, n])
-            keep(t, k, theirs)
-            return carry
-
-        lax.fori_loop(0, KMAX * GROUP, receive, 0)
-
         def receive_side(t, carry):
             landed(side_in.at[t], side_got.at[t])
             return carry
@@ -340,20 +367,25 @@
         def is_home(t):
             return (part == 1) & (home(t) == b)
 
-        def return_zeta(t, n):
-            src = zeta.at[t, pl.ds(HALF * n, HALF)]
-            dst = zeta_in.at[x, pl.ds(HALF * n, HALF)]
-
-            @pl.when(is_home(t))
-            def _():
-                pltpu.make_async_copy(src, dst, zeta_got.at[x, n]).start()
-
-            @pl.when(jnp.logical_not(is_home(t)))
-            def _():
-                pltpu.make_async_remote_copy(
-                    src, dst, zeta_sent.at[t, n], zeta_got.at[x, n],
-                    device_id={"blk": home(t), "sims": plane + part}, device_id_type=MESH,
-                ).start()
+        def return_zeta(rows):
+            def one(step, carry):
+                t = GROUP - 1 - step
+                src, dst = zeta.at[t, rows], zeta_in.at[x, rows]
+
+                @pl.when(is_home(t))
+                def _():
+                    pltpu.make_async_copy(src, dst, zeta_got.at[x]).start()
+
+                @pl.when(jnp.logical_not(is_home(t)))
+                def _():
+                    pltpu.make_async_remote_copy(
+                        src, dst, zeta_sent.at[t], zeta_got.at[x],
+                        device_id={"blk": home(t), "sims": plane + part}, device_id_type=MESH,
+                    ).start()
+
+                return carry
+
+            lax.fori_loop(0, GROUP, one, 0)
 
         def piece(p, carry):
             here = pl.ds(pl.multiple_of(WIDTH * p, WIDTH), WIDTH)
@@ -384,8 +416,7 @@
                 wide = dot(both, push_high[t, 0])
                 low_part = dot(high, push_low[t, 0])
                 update = wide[:WIDTH] + (wide[WIDTH:] + low_part)
-                if t > 0:
-                    far(t, both, high, pending)
+                far(t, both, high, pending)
                 pending[t - 1] = pending[t - 1] + update if t - 1 in pending else update
             edge_out[p, 0] = pending[-1]
 
@@ -393,7 +424,6 @@
             def _():
                 edge_copy(p, 0).start()
 
-            far(0, both, high, pending)
             for d in range(1, 4):
                 edge_out[p, d] = pending[-1 - d]
 
@@ -402,18 +432,19 @@
                 for d in range(1, 4):
                     edge_copy(p, d).start()
 
-            @pl.when(lax.rem(p, PIECES // 2) == PIECES // 2 - 1)
+            @pl.when(is_last)
             def _():
-                def one(step, c):
-                    return_zeta(GROUP - 1 - step, lax.div(p, PIECES // 2))
-                    return c
-
-                lax.fori_loop(0, GROUP, one, 0)
+                return_zeta(here)
 
             return carry
 
         lax.fori_loop(0, early, finish_down, 0)
         lax.fori_loop(0, PIECES, piece, 0)
+
+        @pl.when(jnp.logical_not(is_last))
+        def _():
+            return_zeta(pl.ds(0, COLS))
+
 
         @pl.when(x == 3)
         def _():
@@ -427,16 +458,14 @@
                 for d in range(4):
                     edge_copy(p, d).wait_send()
 
-        def sent_one(step, c):
-            t, n = lax.div(step, 2), lax.rem(step, 2)
-
+        def sent_one(t, c):
             @pl.when(jnp.logical_not(is_home(t)))
             def _():
-                landed(zeta.at[t, pl.ds(HALF * n, HALF)], zeta_sent.at[t, n])
+                landed(zeta.at[t], zeta_sent.at[t])
 
             return c
 
-        lax.fori_loop(0, 2 * GROUP, sent_one, 0)
+        lax.fori_loop(0, GROUP, sent_one, 0)
 
         def passed(t, c):
             for k in range(KMAX):
@@ -448,11 +477,23 @@
 
     exchange(numer, numer_in, numer_sent, numer_got)
 
-    def sent_side(r, carry):
-        sent(r, [(side_out.at[r], side_sent.at[r])])
-        return carry
-
-    lax.fori_loop(0, ROWS, sent_side, 0)
+    @pl.when(core == 0)
+    def _():
+        def sent_side(r, carry):
+            for copy in side_copies(r):
+                copy.wait_send()
+            return carry
+
+        lax.fori_loop(0, ROWS, sent_side, 0)
+
+    @pl.when(core == 1)
+    def _():
+        def sent_twin(r, carry):
+            twin_copy(r).wait_send()
+            return carry
+
+        lax.fori_loop(0, ROWS, sent_twin, 0)
+
     exchanged(denom, denom_in, denom_sent, denom_got)
     exchanged(numer, numer_in, numer_sent, numer_got)
     mean_ref[...] = jnp.sum(numer_in[...], 0) / jnp.sum(denom_in[...], 0)
@@ -468,15 +509,18 @@
             jax.ShapeDtypeStruct((ROWS, BS, COLS), F32),
             jax.ShapeDtypeStruct((SHARE, COLS), F32),
         ),
-        in_specs=[hbm, hbm, pl.BlockSpec(memory_space=pltpu.SMEM), hbm, vmem, vmem],
+        in_specs=[hbm, hbm, pl.BlockSpec(memory_space=pltpu.SMEM), hbm, hbm, hbm],
         out_specs=(vmem, vmem),
         scratch_shapes=[
             pltpu.VMEM((ROWS, BS, COLS), F32),
             pltpu.VMEM((ROWS, KMAX, BS, BS), F32),
             pltpu.VMEM((ROWS, BS, BS), F32),
+            pltpu.VMEM((ROWS, 1, BS), F32),
+            pltpu.VMEM((ROWS, 1, BS), jnp.int32),
             pltpu.VMEM((ROWS, BS, BS), BF16),
             pltpu.VMEM((ROWS, BS, BS), BF16),
             pltpu.VMEM((ROWS, KMAX, BS // 2, BS), F32),
+            pltpu.VMEM((ROWS, COLS + 8, BS), F32),
             pltpu.VMEM((ROWS, COLS + 8, BS), F32),
             pltpu.VMEM((GROUP, KMAX, BS, BS), F32),
             pltpu.VMEM((GROUP, COLS + 8, BS), F32),
@@ -490,9 +534,9 @@
             pltpu.VMEM((NB, SHARE, COLS), F32),
             pltpu.VMEM((NDIST, COLS), F32),
             pltpu.VMEM((NB, SHARE, COLS), F32),
-            dma((ROWS, 3)), dma((ROWS, KMAX)), dma((GROUP, KMAX)), dma((GROUP, KMAX, 2)), dma((GROUP, KMAX, 2)),
-            dma((ROWS,)), dma((GROUP,)), dma((PIECES, 4)), dma((PIECES, 4)),
-            dma((GROUP, 2)), dma((ROWS, 2)),
+            dma((ROWS, 3)), dma((2,)), dma((ROWS, KMAX, 2)), dma((GROUP, KMAX)), dma((GROUP, KMAX, 2)), dma((GROUP, KMAX, 2)),
+            dma((ROWS,)), dma((ROWS,)), dma((ROWS, 2)), dma((GROUP,)), dma((PIECES, 4)), dma((PIECES, 4)),
+            dma((GROUP,)), dma((ROWS,)),
             dma((NB,)), dma((NB,)), dma((NB,)), dma((NB,)),
         ],
         name="back_substitution",
@@ -501,7 +545,7 @@
         ),
     )(
         in_hbm(rhs), in_hbm(lower_blocks), jnp.transpose(col_index, (2, 1, 0)), in_hbm(diag_inverse),
-        turnout, district_of,
+        in_hbm(turnout), in_hbm(district_of),
     )
     return field[:, None], mean
 

time: 96.9 us -> 92.5 us (0.955)
  Pallas kernels: 92.6 us -> 89.7 us
  local copies, waits for them, and re-layouts: 3.44 us -> 2.07 us
    pallas_call x1, Pallas kernels: 92.6 us -> 89.7 us  [body(): pl.pallas_call(kernel, out_shape=(jax.ShapeDtypeStruct((ROWS, BS, COLS),...]
    unnamed x8 -> x4, local copies, waits for them, and re-layouts: 3.44 us -> 2.07 us
where the time goes in v3:
time: 92.5 us; the launch traced here: 92.4 us
  Pallas kernels  89.7 us (97%)
  local copies, waits for them, and re-layouts  2.07 us (2%)
    pallas_call x1, Pallas kernels, body(): pl.pallas_call(kernel, out_shape=(jax.ShapeDtypeStruct((ROWS, BS, COLS),...  89.7 us
    unnamed x4, local copies, waits for them, and re-layouts  2.07 us

profile of v3, /device:TPU:1, one launch (start us, length us, event | category | flops | bytes accessed | tf_op | source)
XLA Modules:
  0.0 92.4 jit_solution(5144846088313802951)
XLA Ops:
  0.6 0.0 copy-start
  0.6 0.7 copy-done
  1.3 89.7 %back_substitution.1 = (f32[4,256,128]{2,1,0:T(8,128)S(1)}, f32[16,128]{1,0:T(8,128)S(1)}) custom-call(f32[4,1,256,128]{3,2,1,0:T(8,128)} %rhs_hbm.1, f32[4,1,3,256,256]{4,3,2,1,0:T(8,128)} %lower_hbm.1, s32[3,1,4]{2,1,0:T(1,128)S(1)} %bitcast.5, f32[4,1,256,256]{3,2,1,0:T(8,128)} %diag_hbm.1, f32[4,1,256]{2,1,0:T(1,128)} %turn_hbm.1, s32[4,1,256]{2,1,0:T(1,128)} %dist_hbm.1), custom_call_target="tpu_custom_call" | custom-call | tf_op jit(solution)/shard_map/back_substitution/pallas_call | solution.py:506
  91.0 0.8 copy.11
  91.8 0.6 copy.12
Async XLA Ops:
  0.6 0.7 copy-start

commit v4 on v3

--- a/solution.py
+++ b/solution.py
@@ -261,6 +261,13 @@
 
     @pl.when(core == 1)
     def _():
+        @pl.when((upper == 1) & (x == 3))
+        def _():
+            edge_out[...] = jnp.zeros_like(edge_out)
+            for p in range(PIECES):
+                for d in range(4):
+                    pltpu.make_async_copy(edge_out.at[p, d], edge_in.at[p, d], edge_got.at[p, d]).start()
+
         for r in range(ROWS):
             twin_copy(r).start()
         forward_all(0)
@@ -337,7 +344,6 @@
     def _():
         half = lax.div(y, 2)
         part = jnp.where(half == 1, lax.rem(y, 2), 1 - lax.rem(y, 2))
-        is_first = (half == 1) & (x == 3)
         is_last = (half == 0) & (x == 0)
         next_b = jnp.where(half == 1, 4 * (1 - part) + x, 4 * (2 + part) + x - 1)
 
@@ -353,13 +359,6 @@
                 edge_out.at[p, d], edge_in.at[p, d], edge_sent.at[p, d], edge_got.at[p, d],
                 device_id={"blk": next_b, "sims": s}, device_id_type=MESH,
             )
-
-        @pl.when(is_first)
-        def _():
-            edge_out[...] = jnp.zeros_like(edge_out)
-            for p in range(PIECES):
-                for d in range(4):
-                    pltpu.make_async_copy(edge_out.at[p, d], edge_in.at[p, d], edge_got.at[p, d]).start()
 
         def home(t):
             return 4 * (2 * half + lax.div(t, 4)) + lax.rem(t, 4)

time: 92.5 us -> 91.9 us (level)
  no operation moved by 1% of the time
where the time goes in v4:
time: 91.9 us; the launch traced here: 91.8 us
  Pallas kernels  89.1 us (97%)
  local copies, waits for them, and re-layouts  2.07 us (2%)
    pallas_call x1, Pallas kernels, body(): pl.pallas_call(kernel, out_shape=(jax.ShapeDtypeStruct((ROWS, BS, COLS),...  89.1 us
    unnamed x4, local copies, waits for them, and re-layouts  2.07 us

profile of v4, /device:TPU:1, one launch (start us, length us, event | category | flops | bytes accessed | tf_op | source)
XLA Modules:
  0.0 91.8 jit_solution(6850415122174584700)
XLA Ops:
  0.6 0.0 copy-start
  0.6 0.7 copy-done
  1.3 89.1 %back_substitution.1 = (f32[4,256,128]{2,1,0:T(8,128)S(1)}, f32[16,128]{1,0:T(8,128)S(1)}) custom-call(f32[4,1,256,128]{3,2,1,0:T(8,128)} %rhs_hbm.1, f32[4,1,3,256,256]{4,3,2,1,0:T(8,128)} %lower_hbm.1, s32[3,1,4]{2,1,0:T(1,128)S(1)} %bitcast.5, f32[4,1,256,256]{3,2,1,0:T(8,128)} %diag_hbm.1, f32[4,1,256]{2,1,0:T(1,128)} %turn_hbm.1, s32[4,1,256]{2,1,0:T(1,128)} %dist_hbm.1), custom_call_target="tpu_custom_call" | custom-call | tf_op jit(solution)/shard_map/back_substitution/pallas_call | solution.py:505
  90.4 0.8 copy.11
  91.2 0.6 copy.12
Async XLA Ops:
  0.6 0.7 copy-start

commit v5 on v4

--- a/solution.py
+++ b/solution.py
@@ -39,9 +39,9 @@
 
 
 def kernel(
-    rhs_hbm, lower_hbm, col_ref, diag_hbm, turn_hbm, dist_hbm,
+    rhs_hbm, lower_hbm, col_hbm, diag_hbm, turn_hbm, dist_hbm,
     sol_ref, mean_ref,
-    rhs_ref, lower_ref, diag_ref, turn_ref, dist_ref,
+    rhs_ref, lower_ref, diag_ref, turn_ref, dist_ref, col_ref,
     diag_high, diag_low, push_out, side_out, side_twin, push_in, side_in, push_high, push_low,
     zeta, zeta_in, edge_in, edge_out, numer, numer_in, denom, denom_in,
     read_got, small_got, push_sent, push_got, pass_sent, pass_got, twin_sent, twin_got, side_sent, side_got, edge_sent, edge_got,
@@ -67,6 +67,8 @@
             copy.start()
         return carry
 
+    columns = pltpu.make_async_copy(col_hbm, col_ref, small_got.at[2])
+    columns.start()
     lax.fori_loop(0, ROWS, start_reads, 0)
     small = (
         pltpu.make_async_copy(turn_hbm, turn_ref, small_got.at[0]),
@@ -226,6 +228,7 @@
         prepare_side(3 - step)
         return carry
 
+    columns.wait()
     lax.fori_loop(0, 1, prepare_sides, 0)
 
     @pl.when(core == 0)
@@ -508,7 +511,7 @@
             jax.ShapeDtypeStruct((ROWS, BS, COLS), F32),
             jax.ShapeDtypeStruct((SHARE, COLS), F32),
         ),
-        in_specs=[hbm, hbm, pl.BlockSpec(memory_space=pltpu.SMEM), hbm, hbm, hbm],
+        in_specs=[hbm, hbm, hbm, hbm, hbm, hbm],
         out_specs=(vmem, vmem),
         scratch_shapes=[
             pltpu.VMEM((ROWS, BS, COLS), F32),
@@ -516,6 +519,7 @@
             pltpu.VMEM((ROWS, BS, BS), F32),
             pltpu.VMEM((ROWS, 1, BS), F32),
             pltpu.VMEM((ROWS, 1, BS), jnp.int32),
+            pltpu.SMEM((KMAX, 1, ROWS), jnp.int32),
             pltpu.VMEM((ROWS, BS, BS), BF16),
             pltpu.VMEM((ROWS, BS, BS), BF16),
             pltpu.VMEM((ROWS, KMAX, BS // 2, BS), F32),
@@ -533,7 +537,7 @@
             pltpu.VMEM((NB, SHARE, COLS), F32),
             pltpu.VMEM((NDIST, COLS), F32),
             pltpu.VMEM((NB, SHARE, COLS), F32),
-            dma((ROWS, 3)), dma((2,)), dma((ROWS, KMAX, 2)), dma((GROUP, KMAX)), dma((GROUP, KMAX, 2)), dma((GROUP, KMAX, 2)),
+            dma((ROWS, 3)), dma((3,)), dma((ROWS, KMAX, 2)), dma((GROUP, KMAX)), dma((GROUP, KMAX, 2)), dma((GROUP, KMAX, 2)),
             dma((ROWS,)), dma((ROWS,)), dma((ROWS, 2)), dma((GROUP,)), dma((PIECES, 4)), dma((PIECES, 4)),
             dma((GROUP,)), dma((ROWS,)),
             dma((NB,)), dma((NB,)), dma((NB,)), dma((NB,)),
@@ -543,7 +547,7 @@
             collective_id=0, has_side_effects=True, vmem_limit_bytes=48 * 1024 * 1024
         ),
     )(
-        in_hbm(rhs), in_hbm(lower_blocks), jnp.transpose(col_index, (2, 1, 0)), in_hbm(diag_inverse),
+        in_hbm(rhs), in_hbm(lower_blocks), in_hbm(jnp.transpose(col_index, (2, 1, 0))), in_hbm(diag_inverse),
         in_hbm(turnout), in_hbm(district_of),
     )
     return field[:, None], mean

time: 91.9 us -> 90.7 us (0.987)
    unnamed x4 -> x2, local copies, waits for them, and re-layouts: 2.07 us -> 1.39 us
where the time goes in v5:
time: 90.7 us; the launch traced here: 90.6 us
  Pallas kernels  88.6 us (98%)
  local copies, waits for them, and re-layouts  1.39 us (2%)
    pallas_call x1, Pallas kernels, body(): pl.pallas_call(kernel, out_shape=(jax.ShapeDtypeStruct((ROWS, BS, COLS),...  88.6 us

profile of v5, /device:TPU:1, one launch (start us, length us, event | category | flops | bytes accessed | tf_op | source)
XLA Modules:
  0.0 90.6 jit_solution(8877901958937653024)
XLA Ops:
  0.6 88.6 %back_substitution.1 = (f32[4,256,128]{2,1,0:T(8,128)S(1)}, f32[16,128]{1,0:T(8,128)S(1)}) custom-call(f32[4,1,256,128]{3,2,1,0:T(8,128)} %rhs_hbm.1, f32[4,1,3,256,256]{4,3,2,1,0:T(8,128)} %lower_hbm.1, s32[3,1,4]{2,1,0:T(1,128)} %bitcast.5, f32[4,1,256,256]{3,2,1,0:T(8,128)} %diag_hbm.1, f32[4,1,256]{2,1,0:T(1,128)} %turn_hbm.1, s32[4,1,256]{2,1,0:T(1,128)} %dist_hbm.1), custom_call_target="tpu_custom_call" | custom-call | tf_op jit(solution)/shard_map/back_substitution/pallas_call | solution.py:508
  89.2 0.8 copy.11
  90.0 0.6 copy.12

commit v6 on v5

--- a/solution.py
+++ b/solution.py
@@ -69,13 +69,11 @@
 
     columns = pltpu.make_async_copy(col_hbm, col_ref, small_got.at[2])
     columns.start()
-    lax.fori_loop(0, ROWS, start_reads, 0)
+    lax.fori_loop(0, 1, start_reads, 0)
     small = (
         pltpu.make_async_copy(turn_hbm, turn_ref, small_got.at[0]),
         pltpu.make_async_copy(dist_hbm, dist_ref, small_got.at[1]),
     )
-    for copy in small:
-        copy.start()
 
     barrier = pltpu.get_barrier_semaphore()
 
@@ -110,6 +108,10 @@
     upper = lax.div(y, 2)
     own_y = jnp.where(upper == 1, 2 + core, 1 - core)
     slot = 4 * lax.rem(y, 2) + x
+
+    lax.fori_loop(1, ROWS, start_reads, 0)
+    for copy in small:
+        copy.start()
 
     def prepare_side(r):
         for copy in reads(r):

time: 90.7 us -> 90.7 us (level)
  no operation moved by 1% of the time
where the time goes in v6:
time: 90.7 us; the launch traced here: 90.6 us
  Pallas kernels  88.5 us (98%)
  local copies, waits for them, and re-layouts  1.39 us (2%)
    pallas_call x1, Pallas kernels, body(): pl.pallas_call(kernel, out_shape=(jax.ShapeDtypeStruct((ROWS, BS, COLS),...  88.5 us

profile of v6, /device:TPU:1, one launch (start us, length us, event | category | flops | bytes accessed | tf_op | source)
XLA Modules:
  0.0 90.6 jit_solution(15587606629315965892)
XLA Ops:
  0.6 88.5 %back_substitution.1 = (f32[4,256,128]{2,1,0:T(8,128)S(1)}, f32[16,128]{1,0:T(8,128)S(1)}) custom-call(f32[4,1,256,128]{3,2,1,0:T(8,128)} %rhs_hbm.1, f32[4,1,3,256,256]{4,3,2,1,0:T(8,128)} %lower_hbm.1, s32[3,1,4]{2,1,0:T(1,128)} %bitcast.5, f32[4,1,256,256]{3,2,1,0:T(8,128)} %diag_hbm.1, f32[4,1,256]{2,1,0:T(1,128)} %turn_hbm.1, s32[4,1,256]{2,1,0:T(1,128)} %dist_hbm.1), custom_call_target="tpu_custom_call" | custom-call | tf_op jit(solution)/shard_map/back_substitution/pallas_call | solution.py:510
  89.2 0.8 copy.11
  90.0 0.6 copy.12
